TPU v7x, 512 devices: a whole 4x8x8 slice. The times are simulated.
512 devices in a mesh: rep: 4 (over z_hi), dp: 16 (over y, core), tensor: 8 (over x, z_lo).
Axes of the slice: x: 4, y: 8, z: 8 (z_hi: 4, z_lo: 2; z = z_hi * 2 + z_lo), core: 2. Of those that a mesh axis runs over, the one named last changes fastest.
Arguments:
- grad_proj: float32 [64, 3072, 1536], P(('rep', 'dp'), 'tensor'), as said below
- grad_conv: float32 [64, 4, 3328], P(('rep', 'dp'), None, 'tensor'), may hold values from -24 to 24
- param_proj: float32 [3072, 1536], P('tensor', 'dp'), may hold values from -6 to 6
- m_proj: float32 [3072, 1536], P('tensor', 'dp'), may hold values from -2 to 2
- v_proj: float32 [3072, 1536], P('tensor', 'dp'), may hold values from 0.02 to 0.2
- ema_proj: float32 [3072, 1536], P(('tensor', 'dp')), may hold values from -6 to 6
- param_conv: float32 [4, 3328], P(None, 'tensor'), may hold values from -3 to 3
- m_conv: float32 [4, 3328], P(None, 'tensor'), may hold values from -2 to 2
- v_conv: float32 [4, 3328], P(None, 'tensor'), may hold values from 0.02 to 0.2
Outputs:
- new_param_proj: float32 [3072, 1536], P('tensor', 'dp')
- new_m_proj: float32 [3072, 1536], P('tensor', 'dp')
- new_v_proj: float32 [3072, 1536], P('tensor', 'dp')
- new_ema_proj: float32 [3072, 1536], P(('tensor', 'dp'))
- weights_proj: bfloat16 [3072, 1536], P('tensor')
- new_param_conv: float32 [4, 3328], P(None, 'tensor')
- new_m_conv: float32 [4, 3328], P(None, 'tensor')
- new_v_conv: float32 [4, 3328], P(None, 'tensor')
Inputs may be any that keep to these rules, and one draw needn't show every extreme that they name: `grad_proj`: Real-valued gradients with entries of magnitude below 3100.
All inputs are finite; a program needn't handle non-finite values.
Results may differ from a plain program's by a relative error of at most 0.001.
Values may be sent and summed in bfloat16 or wider, within the bound.
A program may use at most 64 MiB of HBM per device.

v0:
```python
import math
import jax
import jax.numpy as jnp
from jax import lax
from jax.sharding import PartitionSpec as P

D = 1536
INNER = 3072
CONV = 3328
KCONV = 4


def adamw_step(param_in, first_in, second_in, grad_in):
    first_out = 0.9 * first_in + 0.1 * grad_in
    second_out = 0.95 * second_in + 0.05 * grad_in * grad_in
    bias_one = 1.0 - 0.9**10
    bias_two = 1.0 - 0.95**10
    update = first_out / bias_one / (jnp.sqrt(second_out / bias_two) + 1e-08)
    param_out = param_in - 0.25 * (update + 0.1 * param_in)
    return (param_out, first_out, second_out)


def clip_from(square_sum):
    clip_limit = 0.5 * math.sqrt(INNER * D + KCONV * CONV)
    return jnp.minimum(1.0, clip_limit / (jnp.sqrt(square_sum) + 1e-06))


def body(grad_proj, grad_conv, param_proj, m_proj, v_proj, ema_proj, param_conv, m_conv, v_conv):
    replica_count = lax.axis_size("rep") * lax.axis_size("dp")
    conv_avg = lax.psum(grad_conv[0], ("rep", "dp")) / replica_count
    conv_square = jnp.sum(conv_avg * conv_avg)
    first_owner = lax.axis_index("dp") == 0
    owner_sum = lax.psum_scatter(grad_proj[0], "dp", scatter_dimension=1, tiled=True)
    proj_avg = lax.psum(owner_sum, "rep") / replica_count
    conv_share = jnp.where(first_owner, conv_square, jnp.float32(0.0))
    square_sum = lax.psum(jnp.sum(proj_avg * proj_avg) + conv_share, ("dp", "tensor"))
    clip_factor = clip_from(square_sum)
    new_param_proj, new_m_proj, new_v_proj = adamw_step(
        param_proj, m_proj, v_proj, clip_factor * proj_avg
    )
    new_param_conv, new_m_conv, new_v_conv = adamw_step(
        param_conv, m_conv, v_conv, clip_factor * conv_avg
    )
    ema_count = ema_proj.shape[0]
    full_block = lax.all_gather(
        new_param_proj.astype(jnp.bfloat16), "dp", axis=1, tiled=True
    ).astype(new_param_proj.dtype)
    weights_proj = full_block.astype(jnp.bfloat16)
    row_block = lax.dynamic_slice_in_dim(full_block, lax.axis_index("dp") * ema_count, ema_count, 0)
    new_ema_proj = 0.9 * ema_proj + 0.1 * row_block
    return (
        new_param_proj,
        new_m_proj,
        new_v_proj,
        new_ema_proj,
        weights_proj,
        new_param_conv,
        new_m_conv,
        new_v_conv,
    )


def solution(mesh):
    in_specs = (
        P(("rep", "dp"), "tensor", None),
        P(("rep", "dp"), None, "tensor"),
        P("tensor", "dp"),
        P("tensor", "dp"),
        P("tensor", "dp"),
        P(("tensor", "dp"), None),
        P(None, "tensor"),
        P(None, "tensor"),
        P(None, "tensor"),
    )
    out_specs = (
        P("tensor", "dp"),
        P("tensor", "dp"),
        P("tensor", "dp"),
        P(("tensor", "dp"), None),
        P("tensor", None),
        P(None, "tensor"),
        P(None, "tensor"),
        P(None, "tensor"),
    )
    return jax.shard_map(body, mesh=mesh, in_specs=in_specs, out_specs=out_specs, check_vma=False)
```

profile of v0, /device:TPU:1, one launch (start us, length us, event | category | flops | bytes accessed | tf_op | source)
XLA Modules:
  0.0 549.1 jit_solution(13845586338401462347)
XLA Ops:
  7.2 0.0 reduce-scatter.2.cloned.1.call-start
  7.2 3.1 copy.19
  10.3 0.0 copy-start.8
  10.3 0.0 copy-start.2
  10.3 0.0 copy-start.3
  10.3 0.0 copy-start.4
  10.3 0.0 reduce-scatter.2.cloned.1.call-update
  10.3 0.0 copy-start.1
  10.3 0.0 all-reduce.2.cloned.1.call-start
  10.4 66.1 %reduce-scatter.2.cloned.1.call-done = f32[384,96]{0,1:T(8,128)} async-done(((f32[384,1536]{0,1:T(8,128)}), f32[384,96]{0,1:T(8,128)}) %reduce-scatter.2.cloned.1.call-update) | async-done | bytes 147472 | tf_op jit(solution)/shard_map/reduce_scatter | solution.py:33
  76.5 0.0 all-reduce.2.cloned.1.call-update
  76.5 0.0 copy-start.5
  76.5 0.0 copy-start.6
  76.5 0.0 copy-start.7
  76.5 0.0 all-gather.2.cloned.1.call-start
  76.6 0.0 copy-done.8
  76.6 142.5 %psum.22 = f32[4,416]{1,0:T(4,128)S(1)} all-reduce(f32[4,416]{1,0:T(4,128)S(1)} %bitcast.3), channel_id=1, replica_groups=mesh['rep'=4,'dp'=16,'tensor'=8] {'rep','dp'}, use_global_device_ids=true, to_apply=%region_3.0 | all-reduce | flops 1664 | bytes 13312 | tf_op jit(solution)/shard_map/psum | solution.py:30
  219.1 0.6 multiply_reduce_fusion.1
  220.3 0.0 all-reduce.2.cloned.1.call-done
  220.4 1.6 multiply_reduce_fusion
  222.6 270.7 %psum.23 = f32[]{:T(128)} all-reduce(f32[]{:T(128)S(6)} %add.50), channel_id=1, replica_groups=mesh['rep'=4,'dp'=16,'tensor'=8] {'dp','tensor'}, use_global_device_ids=true, to_apply=%region_5.6 | all-reduce | flops 1 | bytes 8 | tf_op jit(solution)/shard_map/psum | solution.py:36
  494.0 0.0 copy-done.2
  494.0 0.0 copy-done.3
  494.0 0.0 copy-done.4
  494.0 1.8 fusion.3
  495.7 0.0 all-gather.2.cloned.1.call-update
  495.8 0.0 copy-done.1
  495.8 0.3 copy.20
  496.1 0.0 copy-done.5
  496.1 0.0 copy-done.6
  496.1 0.0 copy-done.7
  496.1 0.6 multiply_subtract_fusion.1
  496.7 42.1 %all-gather.2.cloned.1.call-done = bf16[384,1536]{0,1:T(8,128)(2,1)} async-done(((bf16[384,96]{0,1:T(8,128)(2,1)}), bf16[384,1536]{0,1:T(8,128)(2,1)}) %all-gather.2.cloned.1.call-update) | async-done | bytes 1179664 | tf_op jit(solution)/shard_map/all_gather | solution.py:45
  538.8 0.0 copy-start
  538.8 1.4 multiply_add_fusion
  540.3 0.9 copy.21
  541.2 0.0 copy-done
  541.2 1.4 copy.22
Async XLA Ops:
  7.2 69.3 %reduce-scatter.2.cloned.1.call-start = ((), (), s32[]{:S(2)}) async-start(), calls=%async_computation.1 | async-start | bytes 2506752 | tf_op jit(solution)/shard_map/reduce_scatter | solution.py:33
  10.3 66.3 %copy-start.8 = (f32[1,4,416]{2,1,0:T(4,128)S(1)}, f32[1,4,416]{2,1,0:T(4,128)}, u32[]{:S(2)}) copy-start(f32[1,4,416]{2,1,0:T(4,128)} %param.10) | copy-start | bytes 19972
  10.3 483.7 %copy-start.2 = (f32[384,96]{0,1:T(8,128)S(1)}, f32[384,96]{0,1:T(8,128)}, u32[]{:S(2)}) copy-start(f32[384,96]{0,1:T(8,128)} %param.11) | copy-start | bytes 442372
  10.3 483.7 %copy-start.3 = (f32[384,96]{0,1:T(8,128)S(1)}, f32[384,96]{0,1:T(8,128)}, u32[]{:S(2)}) copy-start(f32[384,96]{0,1:T(8,128)} %param.12) | copy-start | bytes 442372
  10.3 483.7 %copy-start.4 = (f32[384,96]{0,1:T(8,128)S(1)}, f32[384,96]{0,1:T(8,128)}, u32[]{:S(2)}) copy-start(f32[384,96]{0,1:T(8,128)} %param.13) | copy-start | bytes 442372
  10.3 485.4 %copy-start.1 = (f32[24,1536]{1,0:T(8,128)S(1)}, f32[24,1536]{1,0:T(8,128)}, u32[]{:S(2)}) copy-start(f32[24,1536]{1,0:T(8,128)} %param.14) | copy-start | bytes 442372
  10.3 210.0 %all-reduce.2.cloned.1.call-start = ((), (), s32[]{:S(2)}) async-start(), calls=%async_computation.2 | async-start | bytes 294912 | tf_op jit(solution)/shard_map/psum | solution.py:34
  76.5 419.6 %copy-start.5 = (f32[4,416]{1,0:T(4,128)S(1)}, f32[4,416]{1,0:T(4,128)}, u32[]{:S(2)}) copy-start(f32[4,416]{1,0:T(4,128)} %param.15) | copy-start | bytes 19972
  76.5 419.5 %copy-start.6 = (f32[4,416]{1,0:T(4,128)S(1)}, f32[4,416]{1,0:T(4,128)}, u32[]{:S(2)}) copy-start(f32[4,416]{1,0:T(4,128)} %param.16) | copy-start | bytes 19972
  76.5 419.5 %copy-start.7 = (f32[4,416]{1,0:T(4,128)S(1)}, f32[4,416]{1,0:T(4,128)}, u32[]{:S(2)}) copy-start(f32[4,416]{1,0:T(4,128)} %param.17) | copy-start | bytes 19972
  76.5 462.3 %all-gather.2.cloned.1.call-start = ((), (), s32[]{:S(2)}) async-start(), calls=%async_computation.3 | async-start | bytes 1253376 | tf_op jit(solution)/shard_map/all_gather | solution.py:45
  538.8 2.3 copy-start
Sparse Core Ops, SparseCore 0:
  10.8 65.6 reduce-scatter.1
  79.4 55.1 all-reduce.1
  495.9 42.8 all-gather.1
where the time goes:
time: 549 us
  blocking collectives  413 us (75%)
  waiting for transfers between devices  108 us (20%)
  between operations  15.9 us (3%)
  other arithmetic  5.98 us (1%)
  local copies, waits for them, and re-layouts  5.74 us (1%)
    psum x1, blocking collectives, body(): lax.psum(jnp.sum(proj_avg * proj_avg) + conv_share, ('dp', 'tensor'))  271 us
    psum x1, blocking collectives, body(): conv_avg = lax.psum(grad_conv[0], ('rep', 'dp')) / replica_count  142 us
    reduce_scatter x1, waiting for transfers between devices, body(): lax.psum_scatter(grad_proj[0], 'dp', scatter_dimension=1, tiled=True)  66.1 us
    all_gather x1, waiting for transfers between devices, body(): lax.all_gather(new_param_proj.astype(jnp.bfloat16), 'dp', axis=1, tiled=T...  42.1 us
  transfers between devices with their start and end apart: 3, of which 2 were waited for; matrix products, arithmetic and copies ran while one was open for 0% of the time, Pallas kernels for 0%

commit v1 on v0

--- a/solution.py
+++ b/solution.py
@@ -27,7 +27,7 @@
 
 def body(grad_proj, grad_conv, param_proj, m_proj, v_proj, ema_proj, param_conv, m_conv, v_conv):
     replica_count = lax.axis_size("rep") * lax.axis_size("dp")
-    conv_avg = lax.psum(grad_conv[0], ("rep", "dp")) / replica_count
+    conv_avg = lax.psum(lax.psum(grad_conv[0], "dp"), "rep") / replica_count
     conv_square = jnp.sum(conv_avg * conv_avg)
     first_owner = lax.axis_index("dp") == 0
     owner_sum = lax.psum_scatter(grad_proj[0], "dp", scatter_dimension=1, tiled=True)

time: 549 us -> 466 us (0.85)
  blocking collectives: 413 us -> 307 us
  waiting for transfers between devices: 108 us -> 131 us
    psum x1 -> x2, blocking collectives: 142 us -> 37.5 us  [body(): conv_avg = lax.psum(lax.psum(grad_conv[0], 'dp'), 'rep') / replica_count]
    psum x1, waiting for transfers between devices: 0.02 us -> 19 us  [body(): proj_avg = lax.psum(owner_sum, 'rep') / replica_count]
  transfers between devices with their start and end apart: 3 -> 3, of which waited for: 2 -> 3; matrix products, arithmetic and copies ran while one was open for 0% -> 0% of each run, Pallas kernels for 0% -> 0%
where the time goes in v1:
time: 466 us
  blocking collectives  307 us (66%)
  waiting for transfers between devices  131 us (28%)
  between operations  15.9 us (3%)
  other arithmetic  5.98 us (1%)
  local copies, waits for them, and re-layouts  5.73 us (1%)
    psum x1, blocking collectives, body(): lax.psum(jnp.sum(proj_avg * proj_avg) + conv_share, ('dp', 'tensor'))  270 us
    reduce_scatter x1, waiting for transfers between devices, body(): lax.psum_scatter(grad_proj[0], 'dp', scatter_dimension=1, tiled=True)  66.1 us
    all_gather x1, waiting for transfers between devices, body(): lax.all_gather(new_param_proj.astype(jnp.bfloat16), 'dp', axis=1, tiled=T...  45.7 us
    psum x2, blocking collectives, body(): conv_avg = lax.psum(lax.psum(grad_conv[0], 'dp'), 'rep') / replica_count  37.5 us
    psum x1, waiting for transfers between devices, body(): proj_avg = lax.psum(owner_sum, 'rep') / replica_count  19 us
  transfers between devices with their start and end apart: 3, of which 3 were waited for; matrix products, arithmetic and copies ran while one was open for 0% of the time, Pallas kernels for 0%

profile of v1, /device:TPU:1, one launch (start us, length us, event | category | flops | bytes accessed | tf_op | source)
XLA Modules:
  0.0 465.9 jit_solution(17850922427320856614)
XLA Ops:
  7.2 0.0 reduce-scatter.2.cloned.1.call-start
  7.2 3.1 copy.19
  10.3 0.0 copy-start.8
  10.3 0.0 copy-start.2
  10.3 0.0 copy-start.3
  10.3 0.0 copy-start.4
  10.3 0.0 reduce-scatter.2.cloned.1.call-update
  10.3 0.0 copy-start.1
  10.3 0.0 all-reduce.2.cloned.1.call-start
  10.4 66.1 %reduce-scatter.2.cloned.1.call-done = f32[384,96]{0,1:T(8,128)} async-done(((f32[384,1536]{0,1:T(8,128)}), f32[384,96]{0,1:T(8,128)}) %reduce-scatter.2.cloned.1.call-update) | async-done | bytes 147472 | tf_op jit(solution)/shard_map/reduce_scatter | solution.py:33
  76.5 0.0 all-reduce.2.cloned.1.call-update
  76.5 0.0 copy-start.5
  76.5 0.0 copy-start.6
  76.5 0.0 copy-start.7
  76.5 0.0 all-gather.2.cloned.1.call-start
  76.6 0.0 copy-done.8
  76.6 25.9 %psum.29 = f32[4,416]{1,0:T(4,128)S(1)} all-reduce(f32[4,416]{1,0:T(4,128)S(1)} %bitcast.3), channel_id=1, replica_groups=mesh['rep'=4,'dp'=16,'tensor'=8] {'dp'}, use_global_device_ids=true, to_apply=%region_3.0 | all-reduce | flops 1664 | bytes 13312 | tf_op jit(solution)/shard_map/psum | solution.py:30
  102.5 11.7 %psum.30 = f32[4,416]{1,0:T(4,128)S(1)} all-reduce(f32[4,416]{1,0:T(4,128)S(1)} %psum.29), channel_id=1, replica_groups=mesh['rep'=4,'dp'=16,'tensor'=8] {'rep'}, use_global_device_ids=true, to_apply=%region_4.0 | all-reduce | flops 1664 | bytes 13312 | tf_op jit(solution)/shard_map/psum | solution.py:30
  114.2 0.6 multiply_reduce_fusion.1
  115.4 19.0 %all-reduce.2.cloned.1.call-done = f32[384,96]{0,1:T(8,128)} async-done(((f32[384,96]{0,1:T(8,128)}), f32[384,96]{0,1:T(8,128)}) %all-reduce.2.cloned.1.call-update) | async-done | bytes 147472 | tf_op jit(solution)/shard_map/psum | solution.py:34
  134.4 1.6 multiply_reduce_fusion
  136.6 269.8 %psum.31 = f32[]{:T(128)} all-reduce(f32[]{:T(128)S(6)} %add.52), channel_id=1, replica_groups=mesh['rep'=4,'dp'=16,'tensor'=8] {'dp','tensor'}, use_global_device_ids=true, to_apply=%region_6.7 | all-reduce | flops 1 | bytes 8 | tf_op jit(solution)/shard_map/psum | solution.py:36
  407.1 0.0 copy-done.2
  407.1 0.0 copy-done.3
  407.1 0.0 copy-done.4
  407.2 1.8 fusion.3
  408.9 0.0 all-gather.2.cloned.1.call-update
  408.9 0.0 copy-done.1
  409.0 0.3 copy.20
  409.2 0.0 copy-done.5
  409.2 0.0 copy-done.6
  409.2 0.0 copy-done.7
  409.3 0.6 multiply_subtract_fusion.1
  409.9 45.7 %all-gather.2.cloned.1.call-done = bf16[384,1536]{0,1:T(8,128)(2,1)} async-done(((bf16[384,96]{0,1:T(8,128)(2,1)}), bf16[384,1536]{0,1:T(8,128)(2,1)}) %all-gather.2.cloned.1.call-update) | async-done | bytes 1179664 | tf_op jit(solution)/shard_map/all_gather | solution.py:45
  455.6 0.0 copy-start
  455.6 1.4 multiply_add_fusion
  457.0 0.9 copy.21
  457.9 0.0 copy-done
  457.9 1.4 copy.22
Async XLA Ops:
  7.2 69.3 %reduce-scatter.2.cloned.1.call-start = ((), (), s32[]{:S(2)}) async-start(), calls=%async_computation.1 | async-start | bytes 2506752 | tf_op jit(solution)/shard_map/reduce_scatter | solution.py:33
  10.3 66.3 %copy-start.8 = (f32[1,4,416]{2,1,0:T(4,128)S(1)}, f32[1,4,416]{2,1,0:T(4,128)}, u32[]{:S(2)}) copy-start(f32[1,4,416]{2,1,0:T(4,128)} %param.10) | copy-start | bytes 19972
  10.3 396.8 %copy-start.2 = (f32[384,96]{0,1:T(8,128)S(1)}, f32[384,96]{0,1:T(8,128)}, u32[]{:S(2)}) copy-start(f32[384,96]{0,1:T(8,128)} %param.11) | copy-start | bytes 442372
  10.3 396.8 %copy-start.3 = (f32[384,96]{0,1:T(8,128)S(1)}, f32[384,96]{0,1:T(8,128)}, u32[]{:S(2)}) copy-start(f32[384,96]{0,1:T(8,128)} %param.12) | copy-start | bytes 442372
  10.3 396.8 %copy-start.4 = (f32[384,96]{0,1:T(8,128)S(1)}, f32[384,96]{0,1:T(8,128)}, u32[]{:S(2)}) copy-start(f32[384,96]{0,1:T(8,128)} %param.13) | copy-start | bytes 442372
  10.3 398.6 %copy-start.1 = (f32[24,1536]{1,0:T(8,128)S(1)}, f32[24,1536]{1,0:T(8,128)}, u32[]{:S(2)}) copy-start(f32[24,1536]{1,0:T(8,128)} %param.14) | copy-start | bytes 442372
  10.3 124.1 %all-reduce.2.cloned.1.call-start = ((), (), s32[]{:S(2)}) async-start(), calls=%async_computation.2 | async-start | bytes 294912 | tf_op jit(solution)/shard_map/psum | solution.py:34
  76.5 332.7 %copy-start.5 = (f32[4,416]{1,0:T(4,128)S(1)}, f32[4,416]{1,0:T(4,128)}, u32[]{:S(2)}) copy-start(f32[4,416]{1,0:T(4,128)} %param.15) | copy-start | bytes 19972
  76.5 332.7 %copy-start.6 = (f32[4,416]{1,0:T(4,128)S(1)}, f32[4,416]{1,0:T(4,128)}, u32[]{:S(2)}) copy-start(f32[4,416]{1,0:T(4,128)} %param.16) | copy-start | bytes 19972
  76.5 332.7 %copy-start.7 = (f32[4,416]{1,0:T(4,128)S(1)}, f32[4,416]{1,0:T(4,128)}, u32[]{:S(2)}) copy-start(f32[4,416]{1,0:T(4,128)} %param.17) | copy-start | bytes 19972
  76.5 379.1 %all-gather.2.cloned.1.call-start = ((), (), s32[]{:S(2)}) async-start(), calls=%async_computation.3 | async-start | bytes 1253376 | tf_op jit(solution)/shard_map/all_gather | solution.py:45
  455.6 2.3 copy-start
Sparse Core Ops, SparseCore 0:
  10.8 65.6 reduce-scatter.1
  79.4 54.9 all-reduce.1
  409.1 46.4 all-gather.1
